TPU v7x, 32 devices: a whole 2x2x4 slice. The times are simulated.
32 devices in a mesh: dp: 8 (over y, x, core), mp: 4 (over z).
Axes of the slice: x: 2, y: 2, z: 4, core: 2. Of those that a mesh axis runs over, the one named last changes fastest.
Arguments:
- tokens: bfloat16 [11264, 768], P('dp'), may hold values from -6 to 6
- lang: int32 [16], P('dp'), may hold values from 0 to 7
- page_len: int32 [16], P('dp'), may hold values from 374 to 561, as said below
- rel_pos: int32 [16, 704, 704], P('dp', 'mp'), may hold values from 0 to 31, as said below
- rel_x: int32 [16, 704, 704], P('dp', 'mp'), may hold values from 0 to 63, as said below
- rel_y: int32 [16, 704, 704], P('dp', 'mp'), may hold values from 0 to 63, as said below
- lang_table: float32 [8, 768], replicated, may hold values from -3 to 3
- convolution_weight: float32 [3, 768], replicated, may hold values from -2.4 to 2.4
- conv_b: float32 [768], replicated, may hold values from -1.8 to 1.8
- w_qkv: bfloat16 [768, 3, 768], P(None, None, 'mp'), may hold values from -0.21875 to 0.21875
- b_qv: float32 [2, 768], P(None, 'mp'), may hold values from -1.8 to 1.8
- bias_table: float32 [160, 12], replicated, may hold values from -3 to 3
- w_out: bfloat16 [768, 768], P('mp'), may hold values from -1.5 to 1.5
- b_out: float32 [768], replicated, may hold values from -1.8 to 1.8
- ln1_gain: float32 [768], replicated, may hold values from 0.5 to 1.5
- ln1_bias: float32 [768], replicated, may hold values from -1.8 to 1.8
- w_in: bfloat16 [768, 3072], P(None, 'mp'), may hold values from -0.21875 to 0.21875
- b_in: float32 [3072], P('mp'), may hold values from -1.8 to 1.8
- w_down: bfloat16 [3072, 768], P('mp'), may hold values from -0.109375 to 0.109375
- b_down: float32 [768], replicated, may hold values from -1.8 to 1.8
- ln2_gain: float32 [768], replicated, may hold values from 0.5 to 1.5
- ln2_bias: float32 [768], replicated, may hold values from -1.8 to 1.8
- cotangent: bfloat16 [11264, 768], P('dp'), may hold values from -6 to 6
Outputs:
- out: bfloat16 [11264, 768], P('dp')
- d_tokens: bfloat16 [11264, 768], P('dp')
- d_lang_table: float32 [8, 768], replicated
- d_conv_w: float32 [3, 768], replicated
- d_conv_b: float32 [768], replicated
- d_w_qkv: float32 [768, 3, 768], P(None, None, 'mp')
- d_b_qv: float32 [2, 768], P(None, 'mp')
- d_bias_table: float32 [160, 12], replicated
- d_w_out: float32 [768, 768], P('mp')
- d_b_out: float32 [768], replicated
- d_ln1_gain: float32 [768], replicated
- d_ln1_bias: float32 [768], replicated
- d_w_in: float32 [768, 3072], P(None, 'mp')
- d_b_in: float32 [3072], P('mp')
- d_w_down: float32 [3072, 768], P('mp')
- d_b_down: float32 [768], replicated
- d_ln2_gain: float32 [768], replicated
- d_ln2_bias: float32 [768], replicated
Inputs may be any that keep to these rules, and one draw needn't show every extreme that they name: `page_len`: the live tokens of a page fill its first slots; one page has exactly 561. `rel_pos`: bucket of the key's reading position minus the query's; positive offsets take the upper 32 // 2 buckets. `rel_x`: bucket of the key's horizontal coordinate minus the query's; positive offsets take the upper 64 // 2 buckets. `rel_y`: bucket of the key's vertical coordinate minus the query's; positive offsets take the upper 64 // 2 buckets.
All inputs are finite; a program needn't handle non-finite values.
Results may differ from a plain program's by a relative error of at most 0.02.
The roundings to bfloat16 on the way count: a program that leaves them out, or rounds other values in their place, can miss the bound.
Values may be sent and summed in bfloat16 or wider, within the bound.
No kernel may reach another device: no remote copies, remote signals or barrier semaphores. Data moves between devices by JAX's collectives and lax.ppermute only.
A program may use at most 256 MiB of HBM per device.

v0:
```python
import math

import jax
import jax.numpy as jnp
from jax import lax
from jax.sharding import PartitionSpec as P

HD = 64
NB1 = 32
NB2 = 64
CONV_TAPS = 3
CONV_DILATION = 2


norm_eps = 1e-05
masked_score = -1000000000.0


def layer_norm(inputs, norm_gain, norm_shift):
    row_mean = jnp.mean(inputs, axis=-1, keepdims=True)
    centred = inputs - row_mean
    spread = jnp.mean(centred * centred, axis=-1, keepdims=True)
    return centred * lax.rsqrt(spread + norm_eps) * norm_gain + norm_shift


def exact_gelu(inputs):
    return jax.nn.gelu(inputs, approximate=False)


def contract_rows(left_side, right_side):
    return lax.dot_general(
        left_side, right_side, (((0,), (0,)), ((), ())), preferred_element_type=jnp.float32
    )


def contract_cols(left_side, right_side):
    return lax.dot_general(
        left_side, right_side, (((1,), (1,)), ((), ())), preferred_element_type=jnp.float32
    )


def bucket_hits(pos_ids, x_ids, y_ids):
    bucket_index = lax.broadcasted_iota(jnp.int32, (NB1 + 2 * NB2, 1), 0)
    first_hit = bucket_index == pos_ids.reshape(1, -1)
    second = bucket_index == x_ids.reshape(1, -1) + NB1
    third_hit = bucket_index == y_ids.reshape(1, -1) + NB1 + NB2
    return first_hit | second | third_hit


def id_blocks(id_array, block_rows):
    page_count, row_count, col_count = id_array.shape
    return id_array.reshape(page_count * row_count // block_rows, block_rows, col_count)


def table_bias(table_rows, pos_ids, x_ids, y_ids):
    page_count, row_count, col_count = pos_ids.shape
    block_rows = math.gcd(row_count, 64)
    head_count = table_rows.shape[0]

    def one_block(pieces):
        bucket_hit = bucket_hits(pieces[0], pieces[1], pieces[2]).astype(jnp.float32)
        looked_up = jnp.dot(table_rows, bucket_hit, precision=lax.Precision.HIGHEST)
        return looked_up.astype(jnp.bfloat16).reshape(head_count, block_rows, col_count)

    blocks = lax.map(
        one_block,
        (
            id_blocks(pos_ids, block_rows),
            id_blocks(x_ids, block_rows),
            id_blocks(y_ids, block_rows),
        ),
    )
    blocks = blocks.reshape(page_count, row_count // block_rows, head_count, block_rows, col_count)
    return jnp.transpose(blocks, (0, 2, 1, 3, 4)).reshape(
        page_count, head_count, row_count, col_count
    )


def table_grad(score_grad, pos_ids, x_ids, y_ids):
    page_count, head_count, row_count, col_count = score_grad.shape
    block_rows = math.gcd(row_count, 64)
    block_count = page_count * row_count // block_rows
    grad_blocks = score_grad.reshape(
        page_count, head_count, row_count // block_rows, block_rows * col_count
    )
    grad_blocks = jnp.transpose(grad_blocks, (0, 2, 1, 3)).reshape(
        block_count, head_count, block_rows * col_count
    )

    def add_block(running, pieces):
        bucket_hit = bucket_hits(pieces[1], pieces[2], pieces[3]).astype(jnp.bfloat16)
        return (running + contract_cols(pieces[0], bucket_hit), None)

    zero_start = jnp.zeros((head_count, NB1 + 2 * NB2), jnp.float32)
    running, unused = lax.scan(
        add_block,
        zero_start,
        (
            grad_blocks,
            id_blocks(pos_ids, block_rows),
            id_blocks(x_ids, block_rows),
            id_blocks(y_ids, block_rows),
        ),
    )
    return running


def body(
    tokens,
    lang,
    page_len,
    rel_pos,
    rel_x,
    rel_y,
    lang_table,
    convolution_weight,
    conv_b,
    w_qkv,
    b_qv,
    bias_table,
    w_out,
    b_out,
    ln1_gain,
    ln1_bias,
    w_in,
    b_in,
    w_down,
    b_down,
    ln2_gain,
    ln2_bias,
    cotangent,
):
    page_count = page_len.shape[0]
    count_of_slots = rel_pos.shape[2]
    model_width = tokens.shape[1]
    local_cols = w_qkv.shape[2]
    heads_here = local_cols // HD
    total_rows = page_count * count_of_slots
    score_scale = HD ** (-0.5)
    slot_index = lax.broadcasted_iota(jnp.int32, (page_count, count_of_slots), 1)
    live_mask = slot_index < page_len[:, None]
    live_rows = live_mask.astype(jnp.float32)[:, :, None]
    key_live = live_mask[:, None, None, :]
    languages = lax.broadcasted_iota(jnp.int32, (1, lang_table.shape[0]), 1)
    lang_pick = (lang[:, None] == languages).astype(jnp.float32)
    convolution_reach = CONV_TAPS // 2 * CONV_DILATION

    def embed(tok_in, lang_weights, kernel_taps, kernel_bias):
        with_lang = (
            tok_in + jnp.dot(lang_pick, lang_weights, precision=lax.Precision.HIGHEST)[:, None, :]
        )
        padded_rows = jnp.pad(
            with_lang * live_rows, ((0, 0), (convolution_reach, convolution_reach), (0, 0))
        )
        convolution_sum = kernel_bias
        for index_of_tap in range(CONV_TAPS):
            convolution_sum = (
                convolution_sum
                + kernel_taps[index_of_tap]
                * padded_rows[
                    :, index_of_tap * CONV_DILATION : index_of_tap * CONV_DILATION + count_of_slots
                ]
            )
        return with_lang + convolution_sum

    tok_in = tokens.astype(jnp.float32).reshape(page_count, count_of_slots, model_width)
    first_pages, embed_back = jax.vjp(embed, tok_in, lang_table, convolution_weight, conv_b)
    first_in = first_pages.reshape(total_rows, model_width)
    first_low = first_in.astype(jnp.bfloat16)
    qkv_flat = w_qkv.reshape(model_width, 3 * local_cols)
    projected = jnp.dot(first_low, qkv_flat, preferred_element_type=jnp.float32).reshape(
        total_rows, 3, local_cols
    )
    head_shape = (page_count, count_of_slots, heads_here, HD)
    queries = (projected[:, 0] + b_qv[0]).astype(jnp.bfloat16).reshape(head_shape)
    key_rows = projected[:, 1].astype(jnp.bfloat16).reshape(head_shape)
    value_rows = (projected[:, 2] + b_qv[1]).astype(jnp.bfloat16).reshape(head_shape)
    row_bias = table_bias(jnp.transpose(bias_table), rel_pos, rel_x, rel_y)
    head_bias = lax.all_to_all(row_bias, "mp", split_axis=1, concat_axis=2, tiled=True)
    scores = (
        jnp.einsum("pqhd,pkhd->phqk", queries, key_rows, preferred_element_type=jnp.float32)
        * score_scale
    )
    scores = jnp.where(key_live, scores + head_bias.astype(jnp.float32), masked_score)
    top_score = jnp.max(scores, axis=-1, keepdims=True)
    exp_scores = jnp.exp(scores - top_score)
    probs_full = exp_scores / jnp.sum(exp_scores, axis=-1, keepdims=True)
    probs_low = probs_full.astype(jnp.bfloat16)
    mixed_heads = jnp.einsum(
        "phqk,pkhd->pqhd", probs_low, value_rows, preferred_element_type=jnp.float32
    )
    mixed_low = mixed_heads.astype(jnp.bfloat16).reshape(total_rows, local_cols)
    attn_part = jnp.dot(mixed_low, w_out, preferred_element_type=jnp.float32)
    attn_sum = lax.psum(attn_part.astype(jnp.bfloat16), "mp").astype(jnp.float32)
    resid_one = first_in + attn_sum + b_out
    hidden_one, norm_one_back = jax.vjp(layer_norm, resid_one, ln1_gain, ln1_bias)
    hidden_low = hidden_one.astype(jnp.bfloat16)
    pre_act = jnp.dot(hidden_low, w_in, preferred_element_type=jnp.float32) + b_in
    activation, gelu_back = jax.vjp(exact_gelu, pre_act)
    activ_low = activation.astype(jnp.bfloat16)
    ffn_part = jnp.dot(activ_low, w_down, preferred_element_type=jnp.float32)
    ffn_sum = lax.psum(ffn_part.astype(jnp.bfloat16), "mp").astype(jnp.float32)
    resid_two = hidden_one + ffn_sum + b_down
    result, norm_two_back = jax.vjp(layer_norm, resid_two, ln2_gain, ln2_bias)
    grad_two, d_ln2_gain, d_ln2_bias = norm_two_back(cotangent.astype(jnp.float32))
    d_b_down = jnp.sum(grad_two, axis=0)
    grad_ffn = grad_two.astype(jnp.bfloat16)
    d_w_down = contract_rows(activ_low, grad_ffn)
    grad_act = contract_cols(grad_ffn, w_down)
    grad_pre = gelu_back(grad_act)[0].astype(jnp.bfloat16)
    d_w_in = contract_rows(hidden_low, grad_pre)
    d_b_in = jnp.sum(grad_pre.astype(jnp.float32), axis=0)
    ffn_back = contract_cols(grad_pre, w_in)
    grad_hidden = grad_two + lax.psum(ffn_back.astype(jnp.bfloat16), "mp").astype(jnp.float32)
    grad_one, d_ln1_gain, d_ln1_bias = norm_one_back(grad_hidden)
    d_b_out = jnp.sum(grad_one, axis=0)
    grad_attn = grad_one.astype(jnp.bfloat16)
    d_w_out = contract_rows(mixed_low, grad_attn)
    grad_mixed = contract_cols(grad_attn, w_out).astype(jnp.bfloat16).reshape(head_shape)
    d_values = jnp.einsum(
        "phqk,pqhd->pkhd", probs_low, grad_mixed, preferred_element_type=jnp.float32
    ).astype(jnp.bfloat16)
    grad_probs = jnp.einsum(
        "pqhd,pkhd->phqk", grad_mixed, value_rows, preferred_element_type=jnp.float32
    )
    grad_scores = probs_full * (
        grad_probs - jnp.sum(probs_full * grad_probs, axis=-1, keepdims=True)
    )
    grad_scores = grad_scores.astype(jnp.bfloat16)
    d_queries = (
        jnp.einsum("phqk,pkhd->pqhd", grad_scores, key_rows, preferred_element_type=jnp.float32)
        * score_scale
    ).astype(jnp.bfloat16)
    d_keys = (
        jnp.einsum("phqk,pqhd->pkhd", grad_scores, queries, preferred_element_type=jnp.float32)
        * score_scale
    ).astype(jnp.bfloat16)
    grad_qkv = jnp.stack([d_queries, d_keys, d_values], axis=2).reshape(total_rows, 3 * local_cols)
    d_w_qkv = contract_rows(first_low, grad_qkv).reshape(model_width, 3, local_cols)
    grad_cols = jnp.sum(grad_qkv.astype(jnp.float32), axis=0).reshape(3, local_cols)
    d_b_qv = jnp.stack([grad_cols[0], grad_cols[2]])
    attn_back = contract_cols(grad_qkv, qkv_flat)
    grad_rows = lax.all_to_all(grad_scores, "mp", split_axis=2, concat_axis=1, tiled=True)
    table_part = jnp.transpose(table_grad(grad_rows, rel_pos, rel_x, rel_y))
    input_sum, d_bias_table = (
        lax.psum(attn_back.astype(jnp.bfloat16), "mp").astype(jnp.float32),
        lax.psum(table_part.astype(jnp.bfloat16), "mp").astype(jnp.float32),
    )
    grad_first = grad_one + input_sum
    d_tokens, d_lang_table, d_conv_w, d_conv_b = embed_back(
        grad_first.reshape(page_count, count_of_slots, model_width)
    )
    (
        d_lang_table,
        d_conv_w,
        d_conv_b,
        d_w_qkv,
        d_b_qv,
        d_bias_table,
        d_w_out,
        d_b_out,
        d_ln1_gain,
        d_ln1_bias,
        d_w_in,
        d_b_in,
        d_w_down,
        d_b_down,
        d_ln2_gain,
        d_ln2_bias,
    ) = lax.psum(
        (
            d_lang_table,
            d_conv_w,
            d_conv_b,
            d_w_qkv,
            d_b_qv,
            d_bias_table,
            d_w_out,
            d_b_out,
            d_ln1_gain,
            d_ln1_bias,
            d_w_in,
            d_b_in,
            d_w_down,
            d_b_down,
            d_ln2_gain,
            d_ln2_bias,
        ),
        "dp",
    )
    return (
        result.astype(jnp.bfloat16),
        d_tokens.reshape(total_rows, model_width).astype(jnp.bfloat16),
        d_lang_table,
        d_conv_w,
        d_conv_b,
        d_w_qkv,
        d_b_qv,
        d_bias_table,
        d_w_out,
        d_b_out,
        d_ln1_gain,
        d_ln1_bias,
        d_w_in,
        d_b_in,
        d_w_down,
        d_b_down,
        d_ln2_gain,
        d_ln2_bias,
    )


def solution(mesh):
    in_specs = (
        P("dp", None),
        P("dp"),
        P("dp"),
        P("dp", "mp", None),
        P("dp", "mp", None),
        P("dp", "mp", None),
        P(),
        P(),
        P(),
        P(None, None, "mp"),
        P(None, "mp"),
        P(),
        P("mp", None),
        P(),
        P(),
        P(),
        P(None, "mp"),
        P("mp"),
        P("mp", None),
        P(),
        P(),
        P(),
        P("dp", None),
    )
    out_specs = (
        P("dp", None),
        P("dp", None),
        P(),
        P(),
        P(),
        P(None, None, "mp"),
        P(None, "mp"),
        P(),
        P("mp", None),
        P(),
        P(),
        P(),
        P(None, "mp"),
        P("mp"),
        P("mp", None),
        P(),
        P(),
        P(),
    )
    return jax.shard_map(body, mesh=mesh, in_specs=in_specs, out_specs=out_specs, check_vma=False)
```

profile of v0, /device:TPU:0, one launch (start us, length us, event | category | flops | bytes accessed | tf_op | source)
XLA Modules:
  0.0 1170.5 jit_solution(16028194539182809648)
XLA Ops:
  7.2 153.9 %while.25 = (s32[]{:T(128)}, bf16[22,12,16,704]{3,2,1,0:T(8,128)(2,1)}, s32[22,16,704]{2,1,0:T(8,128)}, s32[22,16,704]{2,1,0:T(8,128)}, s32[22,16,704]{2,1,0:T(8,128)}, /*index=5*/f32[12,160]{1,0:T(8,128)}, s32[]{:T(128)}) while((s32[]{:T(128)}, bf16[22,12,16,704]{3,2,1,0:T(8,128)(2,1)}, s32[22,16,704]{2,1,0:T(8,128)}, ...), condition=%wide.region_1.2_spmd, body=%wide.region_0.1_spmd.sunk | while | flops 268691456 | bytes 2059873 | solution.py:65
  167.7 6.5 all-to-all-start
  187.6 129.6 %all-to-all-done = bf16[2,12,176,704]{3,2,0,1:T(8,128)(2,1)} async-done(((bf16[2,12,176,704]{3,2,0,1:T(8,128)(2,1)}), bf16[2,12,176,704]{3,2,0,1:T(8,128)(2,1)}, u32[]{:S(2)}, u32[]{:S(2)}) %all-to-all-start) | async-done | bytes 5947424 | tf_op jit(solution)/shard_map/all_to_all | solution.py:179
  320.4 6.2 convert_bitcast_fusion
  326.6 10.5 copy.114
  337.1 14.6 %copy.115 = f32[2,3,704,704]{2,3,1,0:T(8,128)} copy(f32[2,3,704,704]{3,2,1,0:T(8,128)} %bitcast.116) | data formatting | bytes 23789568 | tf_op jit(solution)/shard_map/convert_element_type | solution.py:184
  351.7 9.1 add_select_fusion
  360.9 15.6 %fusion.94 = (f32[2,3,704]{2,1,0:T(4,128)S(1)}, f32[2,3,704,704]{2,3,1,0:T(8,128)}) fusion(f32[2,3,704,704]{2,3,1,0:T(8,128)} %add_select_fusion), kind=kOutput, calls=%fused_computation.168 | output fusion | flops 5948095 | bytes 23806464 | tf_op jit(solution)/shard_map/sub | solution.py:186
  376.4 11.9 %fusion.53 = bf16[2,704,3,64]{1,3,2,0:T(8,128)(2,1)S(1)} fusion(f32[2,704,3,64]{1,0,3,2:T(2,128)} %squeeze.24, f32[3,64]{1,0:T(4,128)S(1)} %add.278, f32[2,3,704]{2,1,0:T(4,128)S(1)} %get-tuple-element.305, f32[2,3,704,704]{2,3,1,0:T(8,128)} %add_select_fusion), kind=kOutput, calls=%fused_computation.115 | convolution fusion | flops 390370112 | bytes 13534464 | tf_op jit(solution)/shard_map/phqk,pkhd->pqhd/dot_general | solution.py:189
  391.6 87.5 %all-reduce.16.cloned.1.call-done = bf16[1408,768]{1,0:T(8,128)(2,1)} async-done(((bf16[1408,768]{1,0:T(8,128)(2,1)}), bf16[1408,768]{1,0:T(8,128)(2,1)}) %all-reduce.16.cloned.1.call-update) | async-done | bytes 2162704 | tf_op jit(solution)/shard_map/psum | solution.py:194
  484.7 12.3 %multiply_convert_fusion.1 = (bf16[1408,768]{1,0:T(8,128)(2,1)S(1)}, f32[1408,768]{1,0:T(8,128)}, f32[1408,768]{1,0:T(8,128)}) fusion(f32[768]{0:T(1024)S(1)} %copy-done.50, bf16[1408,768]{1,0:T(8,128)(2,1)S(1)} %fusion.37, bf16[768,768]{1,0:T(8,128)(2,1)S(1)} %copy-done), kind=kOutput, calls=%fused_computation.69 | convolution fusion | flops 1732313088 | bytes 14158848 | tf_op jit(solution)/shard_map/dot_general | solution.py:198
  501.6 87.4 %all-reduce.18.cloned.1.call-done = bf16[1408,768]{1,0:T(8,128)(2,1)} async-done(((bf16[1408,768]{1,0:T(8,128)(2,1)}), bf16[1408,768]{1,0:T(8,128)(2,1)}) %all-reduce.18.cloned.1.call-update) | async-done | bytes 2162704 | tf_op jit(solution)/shard_map/psum | solution.py:202
  608.5 87.4 %all-reduce.20.cloned.1.call-done = bf16[1408,768]{1,0:T(8,128)(2,1)} async-done(((bf16[1408,768]{1,0:T(8,128)(2,1)}), bf16[1408,768]{1,0:T(8,128)(2,1)}) %all-reduce.20.cloned.1.call-update) | async-done | bytes 2162704 | tf_op jit(solution)/shard_map/psum | solution.py:214
  695.9 6.6 multiply_reduce_fusion.1
  702.5 5.7 fusion.85
  711.9 10.9 multiply_reduce_fusion
  725.0 9.0 multiply_convert_fusion
  734.0 18.2 %copy.125 = bf16[2,3,704,704]{3,0,1,2:T(2,128)(2,1)} copy(bf16[2,3,704,704]{2,3,1,0:T(8,128)(2,1)} %multiply_convert_fusion) | data formatting | bytes 11894784 | tf_op jit(solution)/shard_map/convert_element_type | solution.py:229
  752.1 5.3 all-to-all-start.1
  757.5 11.2 fusion.50
  773.0 4.9 fusion.56
  781.3 5.0 reshape.328
  786.3 4.9 convolution_convert_fusion.2
  791.6 5.2 fusion.96
  796.8 6.4 fusion.78
  810.2 159.6 %all-reduce.22.cloned.1.call-done = bf16[1408,768]{1,0:T(8,128)(2,1)} async-done(((bf16[1408,768]{1,0:T(8,128)(2,1)}), bf16[1408,768]{1,0:T(8,128)(2,1)}) %all-reduce.22.cloned.1.call-update) | async-done | bytes 2162704 | tf_op jit(solution)/shard_map/psum | solution.py:246
  977.1 5.8 multiply_reduce_fusion.3
  990.3 13.8 %reshape.330 = bf16[2,12,11,11264]{3,2,1,0:T(8,128)(2,1)} reshape(bf16[2,4,3,176,704]{4,3,2,1,0:T(8,128)(2,1)} %copy.127) | data formatting | bytes 11894784 | tf_op jit(solution)/shard_map/reshape | solution.py:83
  1004.2 10.4 copy.134
  1014.5 107.7 %while.26 = (s32[]{:T(128)}, f32[12,160]{1,0:T(8,128)S(1)}, bf16[22,12,11264]{2,1,0:T(8,128)(2,1)}, s32[22,16,704]{2,1,0:T(8,128)}, s32[22,16,704]{2,1,0:T(8,128...) while((s32[]{:T(128)}, f32[12,160]{1,0:T(8,128)S(1)}, bf16[22,12,11264]{2,1,0:T(8,128)(2,1)}, ...), condition=%wide.region_29.30_spmd.clone, body=%wide.region_28.29_spmd.clone.sunk | while | flops 52291328 | bytes 1051763 | solution.py:95
  1122.3 9.8 psum.156
  1132.1 23.8 %all-reduce.25 = (f32[8,768]{1,0:T(8,128)}, f32[3,768]{1,0:T(4,128)}, f32[768]{0:T(1024)}, f32[2,192]{1,0:T(2,128)}, f32[160,12]{0,1:T(8,128)}, /*index=5*/f32[7...) all-reduce(f32[8,768]{1,0:T(8,128)S(1)} %fusion.73, ...), channel_id=1, replica_groups=mesh['dp'=8,'mp'=4] {'dp'}, use_global_device_ids=true, to_apply=%region_18.19 | all-reduce | flops 16896 | bytes 131328 | tf_op jit(solution)/shard_map/psum | solution.py:270
  (520 shorter events, 359.8 us)
Async XLA Ops:
  7.2 477.5 %copy-start = (bf16[768,768]{1,0:T(8,128)(2,1)S(1)}, bf16[768,768]{1,0:T(8,128)(2,1)}, u32[]{:S(2)}) copy-start(bf16[768,768]{1,0:T(8,128)(2,1)} %param.43) | copy-start | bytes 3538948
  167.7 7.0 copy-start.39
  167.7 7.1 copy-start.45
  167.7 7.2 copy-start.49
  167.7 7.2 copy-start.51
  167.7 7.4 copy-start.9
  167.7 149.5 %all-to-all-start = ((bf16[2,12,176,704]{3,2,0,1:T(8,128)(2,1)}), bf16[2,12,176,704]{3,2,0,1:T(8,128)(2,1)}, u32[]{:S(2)}, u32[]{:S(2)}) async-start(bf16[2,12,176,704]{3,2,0,1:T(8,128)(2,1)} %copy.112), calls=%async_computation | async-start | bytes 12976128 | tf_op jit(solution)/shard_map/all_to_all | solution.py:179
  174.2 304.9 %all-reduce.16.cloned.1.call-start = ((), (), s32[]{:S(2)}) async-start(), calls=%async_computation.2 | async-start | bytes 4325376 | tf_op jit(solution)/shard_map/psum | solution.py:194
  184.8 166.9 %copy-start.12 = (bf16[2,704,3,64]{1,0,3,2:T(2,128)(2,1)}, bf16[2,704,3,64]{1,0,3,2:T(2,128)(2,1)S(1)}, u32[]{:S(2)}) copy-start(bf16[2,704,3,64]{1,0,3,2:T(2,128)(2,1)S(1)} %convert_element_type.168) | copy-start | bytes 1622020
  187.5 164.2 %copy-start.6 = (f32[2,704,3,64]{1,0,3,2:T(2,128)}, f32[2,704,3,64]{1,0,3,2:T(2,128)S(1)}, u32[]{:S(2)}) copy-start(f32[2,704,3,64]{1,0,3,2:T(2,128)S(1)} %squeeze.25) | copy-start | bytes 3244036
  187.6 164.2 %copy-start.29 = (f32[3,64]{1,0:T(4,128)}, f32[3,64]{1,0:T(4,128)S(1)}, u32[]{:S(2)}) copy-start(f32[3,64]{1,0:T(4,128)S(1)} %add.281) | copy-start | bytes 2308
  376.4 13.0 %copy-start.21 = (bf16[192,768]{1,0:T(8,128)(2,1)S(1)}, bf16[192,768]{1,0:T(8,128)(2,1)}, u32[]{:S(2)}) copy-start(bf16[192,768]{1,0:T(8,128)(2,1)} %param.39) | copy-start | bytes 884740
  388.3 90.8 %copy-start.41 = (f32[768]{0:T(1024)S(1)}, f32[768]{0:T(1024)}, u32[]{:S(2)}) copy-start(f32[768]{0:T(1024)} %param.40) | copy-start | bytes 9220
  389.4 93.2 %copy-start.13 = (bf16[1408,192]{0,1:T(8,128)(2,1)}, bf16[1408,192]{0,1:T(8,128)(2,1)S(1)}, u32[]{:S(2)}) copy-start(bf16[1408,192]{0,1:T(8,128)(2,1)S(1)} %reshape.326) | copy-start | bytes 1622020
  391.6 197.5 %all-reduce.18.cloned.1.call-start = ((), (), s32[]{:S(2)}) async-start(), calls=%async_computation.3 | async-start | bytes 4325376 | tf_op jit(solution)/shard_map/psum | solution.py:202
  484.7 13.6 %copy-start.46 = (bf16[768,768]{1,0:T(8,128)(2,1)S(1)}, bf16[768,768]{1,0:T(8,128)(2,1)}, u32[]{:S(2)}) copy-start(bf16[768,768]{1,0:T(8,128)(2,1)} %param.45) | copy-start | bytes 3538948
  498.3 90.7 %copy-start.40 = (f32[768]{0:T(1024)S(1)}, f32[768]{0:T(1024)}, u32[]{:S(2)}) copy-start(f32[768]{0:T(1024)} %param.46) | copy-start | bytes 9220
  501.6 194.3 %all-reduce.20.cloned.1.call-start = ((), (), s32[]{:S(2)}) async-start(), calls=%async_computation.4 | async-start | bytes 4325376 | tf_op jit(solution)/shard_map/psum | solution.py:214
  702.5 7.8 copy-start.22
  711.8 10.9 slice-start
  711.8 12.0 %slice-start.1 = ((s8[12976128]{0:T(1024)(128)(4,1)}), s8[4194304]{0:T(1024)(128)(4,1)S(1)}, s32[]{:S(2)}) async-start(s8[12976128]{0:T(1024)(128)(4,1)} %bitcast.117), calls=%async_computation.8 | async-start | bytes 8388608
  711.8 13.2 %slice-start.2 = ((s8[12976128]{0:T(1024)(128)(4,1)}), s8[4194304]{0:T(1024)(128)(4,1)S(1)}, s32[]{:S(2)}) async-start(s8[12976128]{0:T(1024)(128)(4,1)} %bitcast.117), calls=%async_computation.9 | async-start | bytes 8388608
  711.8 13.2 %slice-start.3 = ((s8[12976128]{0:T(1024)(128)(4,1)}), s8[393216]{0:T(1024)(128)(4,1)S(1)}, s32[]{:S(2)}) async-start(s8[12976128]{0:T(1024)(128)(4,1)} %bitcast.117), calls=%async_computation.10 | async-start | bytes 786432
  752.1 231.2 %all-to-all-start.1 = ((bf16[2,3,704,704]{3,0,1,2:T(2,128)(2,1)}), bf16[2,3,704,704]{3,0,1,2:T(2,128)(2,1)}, u32[]{:S(2)}, u32[]{:S(2)}) async-start(bf16[2,3,704,704]{3,0,1,2:T(2,128)(2,1)} %copy.125), calls=%async_computation.1 | async-start | bytes 12976128 | tf_op jit(solution)/shard_map/all_to_all | solution.py:243
  757.4 212.4 %all-reduce.22.cloned.1.call-start = ((), (), s32[]{:S(2)}) async-start(), calls=%async_computation.5 | async-start | bytes 4325376 | tf_op jit(solution)/shard_map/psum | solution.py:246
  791.2 364.6 %all-reduce.24.cloned.1.call-start = ((), (), s32[]{:S(2)}) async-start(), calls=%async_computation.6 | async-start | bytes 14155776 | tf_op jit(solution)/shard_map/psum | solution.py:270
  810.1 159.7 %copy-start.10 = (bf16[1408,768]{1,0:T(8,128)(2,1)S(1)}, bf16[1408,768]{1,0:T(8,128)(2,1)}, u32[]{:S(2)}) copy-start(bf16[1408,768]{1,0:T(8,128)(2,1)} %param.27) | copy-start | bytes 6488068
  810.1 159.7 %copy-start.28 = (f32[2,768]{1,0:T(2,128)S(1)}, f32[2,768]{1,0:T(2,128)}, u32[]{:S(2)}) copy-start(f32[2,768]{1,0:T(2,128)} %copy-done.27) | copy-start | bytes 18436
  810.1 164.2 %copy-start.32 = (f32[768]{0:T(1024)S(1)}, f32[768]{0:T(1024)}, u32[]{:S(2)}) copy-start(f32[768]{0:T(1024)} %copy-done.31) | copy-start | bytes 9220
  810.1 164.2 %copy-start.34 = (f32[768]{0:T(1024)S(1)}, f32[768]{0:T(1024)}, u32[]{:S(2)}) copy-start(f32[768]{0:T(1024)} %copy-done.33) | copy-start | bytes 9220
  810.1 164.2 %copy-start.36 = (f32[768]{0:T(1024)S(1)}, f32[768]{0:T(1024)}, u32[]{:S(2)}) copy-start(f32[768]{0:T(1024)} %copy-done.35) | copy-start | bytes 9220
  969.8 7.4 slice-start.4
  (40 other events, 126.1 us)
Sparse Core Ops, SparseCore 0:
  391.7 87.3 all-reduce.15
  501.7 87.2 all-reduce.17
  608.6 87.2 all-reduce.19
  791.3 178.3 all-reduce.21
  974.5 111.7 all-reduce.23
where the time goes:
time: 1180 us; the launch traced here: 1170 us
  waiting for transfers between devices  552 us (47%)
  matrix products  255 us (22%)
  local copies, waits for them, and re-layouts  189 us (16%)
  other arithmetic  113 us (10%)
  blocking collectives  33.6 us (3%)
  between operations  14.9 us (1%)
  starting transfers between devices  12.7 us (1%)
    psum x1, waiting for transfers between devices, body(): lax.psum(attn_back.astype(jnp.bfloat16), 'mp').astype(jnp.float32)  160 us
    all_to_all x1, waiting for transfers between devices, body(): lax.all_to_all(row_bias, 'mp', split_axis=1, concat_axis=2, tiled=True)  130 us
    psum x1, waiting for transfers between devices, body(): lax.psum(attn_part.astype(jnp.bfloat16), 'mp').astype(jnp.float32)  87.5 us
    psum x1, waiting for transfers between devices, body(): lax.psum(ffn_back.astype(jnp.bfloat16), 'mp').astype(jnp.float32)  87.4 us
    psum x1, waiting for transfers between devices, body(): ffn_sum = lax.psum(ffn_part.astype(jnp.bfloat16), 'mp').astype(jnp.float32)  87.4 us
    dot_general x22, matrix products, one_block(): looked_up = jnp.dot(table_rows, bucket_hit, precision=lax.Precision.HIGHEST)  86.8 us
    dot_general x26, matrix products, contract_cols(): lax.dot_general(left_side, right_side, (((1,), (1,)), ((), ())), preferre...  78.4 us
    add x44, other arithmetic, bucket_hits(): third_hit = bucket_index == y_ids.reshape(1, -1) + NB1 + NB2  36.8 us
  transfers between devices with their start and end apart: 7, of which 5 were waited for; matrix products, arithmetic and copies ran while one was open for 19% of the time, Pallas kernels for 0%

commit v1 on v0

v1 whole, which is shorter than its diff:
```python
import functools

import jax
import jax.numpy as jnp
from jax import lax
from jax.experimental import pallas as pl
from jax.experimental.pallas import tpu as pltpu
from jax.sharding import PartitionSpec as P

HD = 64
NB1 = 32
NB2 = 64
CONV_TAPS = 3
CONV_DILATION = 2
PAGE_MAX = 561
LANES = 128
KEYS = -(-PAGE_MAX // LANES) * LANES
CHUNK = 16

norm_eps = 1e-05
masked_score = -1000000000.0
bf16 = jnp.bfloat16
f32 = jnp.float32


def layer_norm(inputs, norm_gain, norm_shift):
    row_mean = jnp.mean(inputs, axis=-1, keepdims=True)
    centred = inputs - row_mean
    spread = jnp.mean(centred * centred, axis=-1, keepdims=True)
    return centred * lax.rsqrt(spread + norm_eps) * norm_gain + norm_shift


def exact_gelu(inputs):
    return jax.nn.gelu(inputs, approximate=False)


def dot_nt(a, b):
    return lax.dot_general(a, b, (((1,), (1,)), ((), ())), preferred_element_type=f32)


def dot_nn(a, b):
    return lax.dot_general(a, b, (((1,), (0,)), ((), ())), preferred_element_type=f32)


def dot_tn(a, b):
    return lax.dot_general(a, b, (((0,), (0,)), ((), ())), preferred_element_type=f32)


def attn_fwd_kernel(len_ref, q_ref, k_ref, v_ref, pos_ref, x_ref, y_ref, tab_ref,
                    mixed_ref, p_ref, s_ref, pb_ref):
    page = pl.program_id(0)
    pair = pl.program_id(1)
    rows = q_ref.shape[0]
    length = len_ref[page]
    lane = lax.broadcasted_iota(jnp.int32, (rows, LANES), 1)
    q = q_ref[...]
    k = k_ref[0]
    v = v_ref[0]
    outs = []
    for sub in range(2):
        mine = (lane >= HD) if sub else (lane < HD)
        s_ref[sub] = dot_nt(jnp.where(mine, q, jnp.zeros_like(q)), k)
        head = pair * 2 + sub
        tabs = [
            jnp.broadcast_to(tab_ref[t, pl.ds(head, 1), :], (CHUNK, LANES)) for t in range(3)
        ]

        def chunk(c, carry, sub=sub, tabs=tabs):
            at = pl.ds(pl.multiple_of(c * CHUNK, CHUNK), CHUNK)
            pieces = []
            for b in range(KEYS // LANES):
                cols = slice(b * LANES, (b + 1) * LANES)
                bias = None
                for tab, ids in zip(tabs, (pos_ref, x_ref, y_ref)):
                    got = jnp.take_along_axis(
                        tab, ids[0, at, cols], axis=1, mode="promise_in_bounds"
                    )
                    bias = got if bias is None else bias + got
                col = lax.broadcasted_iota(jnp.int32, (CHUNK, LANES), 1) + b * LANES
                val = s_ref[sub, at, cols] + bias.astype(bf16).astype(f32)
                pieces.append(jnp.where(col < length, val, masked_score))
            top = functools.reduce(jnp.maximum, pieces)
            top = jnp.max(top, axis=1, keepdims=True)
            es = [jnp.exp(piece - top) for piece in pieces]
            total = jnp.sum(functools.reduce(jnp.add, es), axis=1, keepdims=True)
            inv = 1.0 / total
            for b, e in enumerate(es):
                cols = slice(b * LANES, (b + 1) * LANES)
                prob = e * inv
                p_ref[0, sub, at, cols] = prob
                pb_ref[sub, at, cols] = prob.astype(bf16)
            return carry

        lax.fori_loop(0, rows // CHUNK, chunk, 0, unroll=True)
        outs.append(dot_nn(pb_ref[sub], v))
    mixed_ref[...] = jnp.where(lane < HD, outs[0], outs[1]).astype(bf16)


def attn_bwd_kernel(q_ref, k_ref, v_ref, gm_ref, p_ref, pos_ref, x_ref, y_ref,
                    dq_ref, dk_ref, dv_ref, tab_ref, dp_ref, pb_ref, ds_ref, all_ref):
    page = pl.program_id(0)
    pair = pl.program_id(1)
    rows = q_ref.shape[0]
    heads = 2 * pl.num_programs(1)
    lane = lax.broadcasted_iota(jnp.int32, (rows, LANES), 1)
    q = q_ref[...]
    gm = gm_ref[...]
    k = k_ref[0]
    v = v_ref[0]
    dk = dv = None
    dqs = []
    for sub in range(2):
        mine = (lane >= HD) if sub else (lane < HD)
        qm = jnp.where(mine, q, jnp.zeros_like(q))
        gmm = jnp.where(mine, gm, jnp.zeros_like(gm))
        dp_ref[sub] = dot_nt(gmm, v)
        base = (pair * 2 + sub) * rows

        def chunk(c, carry, sub=sub, base=base):
            at = pl.ds(pl.multiple_of(c * CHUNK, CHUNK), CHUNK)
            to = pl.ds(pl.multiple_of(base + c * CHUNK, CHUNK), CHUNK)
            ps = []
            dps = []
            acc = None
            for b in range(KEYS // LANES):
                cols = slice(b * LANES, (b + 1) * LANES)
                ps.append(p_ref[0, sub, at, cols])
                dps.append(dp_ref[sub, at, cols])
                prod = ps[-1] * dps[-1]
                acc = prod if acc is None else acc + prod
            mean = jnp.sum(acc, axis=1, keepdims=True)
            for b in range(KEYS // LANES):
                cols = slice(b * LANES, (b + 1) * LANES)
                ds = (ps[b] * (dps[b] - mean)).astype(bf16)
                pb_ref[sub, at, cols] = ps[b].astype(bf16)
                ds_ref[sub, at, cols] = ds
                all_ref[b, to, :] = ds.astype(f32)
            return carry

        lax.fori_loop(0, rows // CHUNK, chunk, 0, unroll=True)
        dqs.append(dot_nn(ds_ref[sub], k))
        dkh = dot_tn(ds_ref[sub], qm)
        dvh = dot_tn(pb_ref[sub], gmm)
        dk = dkh if dk is None else dk + dkh
        dv = dvh if dv is None else dv + dvh
    dq_ref[...] = (jnp.where(lane < HD, dqs[0], dqs[1]) * HD ** -0.5).astype(bf16)
    dk_ref[0] = dk.astype(bf16)
    dv_ref[0] = dv.astype(bf16)

    @pl.when((page == 0) & (pair == 0))
    def _():
        tab_ref[...] = jnp.zeros_like(tab_ref)

    @pl.when(pair == pl.num_programs(1) - 1)
    def _():
        nheads = tab_ref.shape[1]

        def row(i, accs):
            g = jnp.concatenate(
                [all_ref[b, pl.ds(i, nheads, stride=rows), :] for b in range(KEYS // LANES)],
                axis=1,
            ).astype(bf16)
            new = []
            for acc, ids, count in zip(accs, (pos_ref, x_ref, y_ref), (NB1, NB2, NB2)):
                idr = ids[0, pl.ds(i, 1), :].astype(f32).astype(bf16)
                bucket = lax.broadcasted_iota(jnp.int32, (count, KEYS), 0).astype(f32).astype(bf16)
                hit = jnp.where(bucket == idr, jnp.ones((), bf16), jnp.zeros((), bf16))
                new.append(acc + dot_nt(hit, g))
            return tuple(new)

        accs = tuple(jnp.zeros((c, nheads), f32) for c in (NB1, NB2, NB2))
        accs = lax.fori_loop(0, rows, row, accs, unroll=4)
        tab_ref[0:NB1, :] += accs[0]
        tab_ref[NB1 : NB1 + NB2, :] += accs[1]
        tab_ref[NB1 + NB2 : NB1 + 2 * NB2, :] += accs[2]


def attn_specs(rows):
    qs = pl.BlockSpec((rows, LANES), lambda p, h, *_: (p, h))
    ks = pl.BlockSpec((1, KEYS, LANES), lambda p, h, *_: (p, 0, h))
    ids = pl.BlockSpec((1, rows, KEYS), lambda p, h, *_: (p, 0, 0))
    ps = pl.BlockSpec((1, 2, rows, KEYS), lambda p, h, *_: (p, h, 0, 0))
    return qs, ks, ids, ps


def attn_fwd(page_len, q, k, v, pos, x, y, tab):
    pages, rows, _ = pos.shape
    heads = q.shape[1] // HD
    qs, ks, ids, ps = attn_specs(rows)
    return pl.pallas_call(
        attn_fwd_kernel,
        out_shape=(
            jax.ShapeDtypeStruct(q.shape, bf16),
            jax.ShapeDtypeStruct((pages, heads, rows, KEYS), f32),
        ),
        grid_spec=pltpu.PrefetchScalarGridSpec(
            num_scalar_prefetch=1,
            grid=(pages, heads // 2),
            in_specs=[qs, ks, ks, ids, ids, ids,
                      pl.BlockSpec(tab.shape, lambda p, h, *_: (0, 0, 0))],
            out_specs=(qs, ps),
            scratch_shapes=[pltpu.VMEM((2, rows, KEYS), f32), pltpu.VMEM((2, rows, KEYS), bf16)],
        ),
    )(page_len, q, k, v, pos, x, y, tab)


def attn_bwd(q, k, v, gm, p, pos, x, y):
    pages, rows, _ = pos.shape
    heads = q.shape[1] // HD
    qs, ks, ids, ps = attn_specs(rows)
    kv = jax.ShapeDtypeStruct(k.shape, bf16)
    return pl.pallas_call(
        attn_bwd_kernel,
        out_shape=(
            jax.ShapeDtypeStruct(q.shape, bf16), kv, kv,
            jax.ShapeDtypeStruct((NB1 + 2 * NB2, heads), f32),
        ),
        grid=(pages, heads // 2),
        in_specs=[qs, ks, ks, qs, ps, ids, ids, ids],
        out_specs=(qs, ks, ks, pl.BlockSpec((NB1 + 2 * NB2, heads), lambda p, h: (0, 0))),
        scratch_shapes=[
            pltpu.VMEM((2, rows, KEYS), f32),
            pltpu.VMEM((2, rows, KEYS), bf16),
            pltpu.VMEM((2, rows, KEYS), bf16),
            pltpu.VMEM((KEYS // LANES, heads * rows, LANES), f32),
        ],
    )(q, k, v, gm, p, pos, x, y)


def body(tokens, lang, page_len, rel_pos, rel_x, rel_y, lang_table, convolution_weight, conv_b,
         w_qkv, b_qv, bias_table, w_out, b_out, ln1_gain, ln1_bias, w_in, b_in, w_down, b_down,
         ln2_gain, ln2_bias, cotangent, *, n_dp, n_mp):
    dp = lax.axis_index("dp")
    mp = lax.axis_index("mp")
    page_count = page_len.shape[0]
    rows = rel_pos.shape[1]
    slots = rel_pos.shape[2]
    width = tokens.shape[1]
    cols = w_qkv.shape[2]
    units = w_in.shape[1]
    own_rows = page_count * rows
    score_scale = HD ** (-0.5)

    def share(w):
        step = w.shape[0] // n_dp
        return lax.dynamic_slice_in_dim(w, dp * step, step, 0)

    in_all = lax.all_gather(share(w_in), ("mp", "dp"), axis=0, tiled=True)
    down_all = lax.all_gather(share(w_down), ("mp", "dp"), axis=0, tiled=True)
    in_all = in_all.reshape(n_mp, width, units)
    down_all = down_all.reshape(n_mp, units, width)

    def spread(block, paired):
        half = block.shape[0] // 2
        odd = dp % 2
        sent = lax.dynamic_slice_in_dim(block, odd * half, half, 0) if paired else block
        got = [
            lax.ppermute(sent, "mp", [(i, (i + s) % n_mp) for i in range(n_mp)])
            for s in range(1, n_mp)
        ]
        if paired:
            mate = [(i, i ^ 1) for i in range(n_dp)]
            other = [lax.ppermute(g, "dp", mate) for g in got]
            got = [
                jnp.concatenate([jnp.where(odd == 0, g, o), jnp.where(odd == 0, o, g)], axis=0)
                for g, o in zip(got, other)
            ]
        line = jnp.stack([block] + got)
        order = (mp - jnp.arange(n_mp)) % n_mp
        return jnp.take(line, order, axis=0, mode="clip")

    qkv_t = jnp.transpose(w_qkv.reshape(width, 3 * cols))
    paired = n_dp % 2 == 0
    attn_w = spread(jnp.concatenate([qkv_t, w_out], axis=0), paired)
    wq_t, wk_t, wv_t, wo = [
        attn_w[:, t * cols : (t + 1) * cols].reshape(n_mp * cols, width) for t in range(4)
    ]
    small = spread(jnp.concatenate([b_in, b_qv.reshape(-1)]).reshape(-1, LANES), False)
    small = small.reshape(n_mp, units + 2 * cols)
    bin_all = small[:, :units]
    bq = small[:, units : units + cols].reshape(-1)
    bv = small[:, units + cols :].reshape(-1)

    slot_index = lax.broadcasted_iota(jnp.int32, (page_count, slots), 1)
    live_rows = (slot_index < page_len[:, None]).astype(f32)[:, :, None]
    languages = lax.broadcasted_iota(jnp.int32, (1, lang_table.shape[0]), 1)
    lang_pick = (lang[:, None] == languages).astype(f32)
    convolution_reach = CONV_TAPS // 2 * CONV_DILATION

    def embed(tok_in, lang_weights, kernel_taps, kernel_bias):
        with_lang = (
            tok_in + jnp.dot(lang_pick, lang_weights, precision=lax.Precision.HIGHEST)[:, None, :]
        )
        padded_rows = jnp.pad(
            with_lang * live_rows, ((0, 0), (convolution_reach, convolution_reach), (0, 0))
        )
        convolution_sum = kernel_bias
        for index_of_tap in range(CONV_TAPS):
            convolution_sum = (
                convolution_sum
                + kernel_taps[index_of_tap]
                * padded_rows[
                    :, index_of_tap * CONV_DILATION : index_of_tap * CONV_DILATION + slots
                ]
            )
        return with_lang + convolution_sum

    def own(a):
        return lax.dynamic_slice_in_dim(a, mp * rows, rows, 1).reshape(own_rows, a.shape[2])

    tok_in = tokens.astype(f32).reshape(page_count, slots, width)
    first_pages, embed_back = jax.vjp(embed, tok_in, lang_table, convolution_weight, conv_b)
    first_own = own(first_pages)
    first_own_low = first_own.astype(bf16)
    first_keys = first_pages[:, :KEYS].astype(bf16).reshape(page_count * KEYS, width)
    queries = ((dot_nt(first_own_low, wq_t) + bq).astype(bf16) * score_scale).astype(bf16)
    key_rows = dot_nt(first_keys, wk_t).astype(bf16).reshape(page_count, KEYS, width)
    value_rows = (dot_nt(first_keys, wv_t) + bv).astype(bf16).reshape(page_count, KEYS, width)
    table_t = jnp.transpose(bias_table)
    tab = jnp.stack([
        jnp.pad(t, ((0, 0), (0, LANES - t.shape[1])))
        for t in (table_t[:, :NB1], table_t[:, NB1 : NB1 + NB2], table_t[:, NB1 + NB2 :])
    ])
    mixed_low, probs = attn_fwd(page_len, queries, key_rows, value_rows, rel_pos, rel_x, rel_y, tab)
    attn_sum = 0.0
    for g in range(n_mp):
        part = dot_nn(mixed_low[:, g * cols : (g + 1) * cols], wo[g * cols : (g + 1) * cols])
        attn_sum = attn_sum + part.astype(bf16).astype(f32)
    resid_one = first_own + attn_sum + b_out
    hidden_one, norm_one_back = jax.vjp(layer_norm, resid_one, ln1_gain, ln1_bias)
    hidden_low = hidden_one.astype(bf16)
    ffn_sum = 0.0
    acts = []
    for g in range(n_mp):
        pre_act = dot_nn(hidden_low, in_all[g]) + bin_all[g]
        activation, gelu_back = jax.vjp(exact_gelu, pre_act)
        activ_low = activation.astype(bf16)
        acts.append((activ_low, gelu_back))
        ffn_sum = ffn_sum + dot_nn(activ_low, down_all[g]).astype(bf16).astype(f32)
    resid_two = hidden_one + ffn_sum + b_down
    result, norm_two_back = jax.vjp(layer_norm, resid_two, ln2_gain, ln2_bias)
    out_own = result.astype(bf16).reshape(page_count, rows, width)

    cot_own = own(cotangent.reshape(page_count, slots, width)).astype(f32)
    grad_two, d_ln2_gain, d_ln2_bias = norm_two_back(cot_own)
    d_b_down = jnp.sum(grad_two, axis=0)
    grad_ffn = grad_two.astype(bf16)
    grad_hidden = grad_two
    d_in = []
    d_down = []
    d_bin = []
    for g in range(n_mp):
        activ_low, gelu_back = acts[g]
        d_down.append(dot_tn(activ_low, grad_ffn).astype(bf16))
        grad_pre = gelu_back(dot_nt(grad_ffn, down_all[g]))[0].astype(bf16)
        d_in.append(dot_tn(hidden_low, grad_pre).astype(bf16))
        d_bin.append(jnp.sum(grad_pre.astype(f32), axis=0))
        grad_hidden = grad_hidden + dot_nt(grad_pre, in_all[g])
    grad_one, d_ln1_gain, d_ln1_bias = norm_one_back(grad_hidden)
    d_b_out = jnp.sum(grad_one, axis=0)
    grad_attn = grad_one.astype(bf16)
    grad_mixed = dot_nt(grad_attn, wo).astype(bf16)
    d_queries, d_keys, d_values, table_part = attn_bwd(
        queries, key_rows, value_rows, grad_mixed, probs, rel_pos, rel_x, rel_y
    )
    dk_flat = d_keys.reshape(page_count * KEYS, width)
    dv_flat = d_values.reshape(page_count * KEYS, width)

    own_part = (grad_one + dot_nn(d_queries, wq_t)).reshape(page_count, rows, width)
    key_part = (dot_nn(dk_flat, wk_t) + dot_nn(dv_flat, wv_t)).reshape(page_count, KEYS, width)
    grad_first = jnp.pad(key_part, ((0, 0), (0, slots - KEYS), (0, 0)))
    grad_first = lax.dynamic_update_slice_in_dim(
        grad_first,
        lax.dynamic_slice_in_dim(grad_first, mp * rows, rows, 1) + own_part,
        mp * rows,
        1,
    )
    d_tokens, d_lang_table, d_conv_w, d_conv_b = embed_back(grad_first)
    d_tokens = lax.psum(d_tokens.astype(bf16), "mp")

    out = lax.all_gather(out_own, "mp", axis=1, tiled=True)

    ffn_parts = jnp.concatenate(
        [jnp.stack(d_in), jnp.stack(d_down)], axis=0
    ).reshape(2 * n_mp, n_dp, width // n_dp, units)
    attn_parts = jnp.stack([
        dot_tn(first_own_low, d_queries).astype(bf16),
        dot_tn(first_keys, dk_flat).astype(bf16),
        dot_tn(first_keys, dv_flat).astype(bf16),
        dot_tn(grad_attn, mixed_low).astype(bf16),
    ]).reshape(4, n_dp, width // n_dp, n_mp * cols)
    ffn_parts = jnp.transpose(ffn_parts, (1, 0, 2, 3))
    attn_parts = jnp.transpose(attn_parts, (1, 0, 2, 3))
    ffn_parts = lax.psum_scatter(ffn_parts, "dp", scatter_dimension=0, tiled=False)
    attn_parts = lax.psum_scatter(attn_parts, "dp", scatter_dimension=0, tiled=False)
    ffn_parts = ffn_parts.reshape(2, n_mp, width // n_dp, units)
    ffn_parts = jnp.transpose(ffn_parts, (1, 0, 2, 3)).reshape(n_mp, -1, LANES)
    attn_parts = attn_parts.reshape(4 * (width // n_dp), n_mp, cols)
    attn_parts = jnp.transpose(attn_parts, (1, 0, 2)).reshape(n_mp, -1, LANES)
    split = ffn_parts.shape[1]
    shares = lax.psum_scatter(
        jnp.concatenate([ffn_parts, attn_parts], axis=1), "mp", scatter_dimension=0, tiled=False
    )
    blocks = lax.all_gather(shares, "dp", axis=0, tiled=False).astype(f32)
    ffn_blocks = blocks[:, :split].reshape(n_dp, 2, width // n_dp, units)
    d_w_in, d_w_down = [ffn_blocks[:, t].reshape(width, units) for t in range(2)]
    attn_blocks = blocks[:, split:].reshape(n_dp, 4, width // n_dp, cols)
    attn_blocks = jnp.transpose(attn_blocks, (1, 0, 2, 3)).reshape(4, width, cols)
    d_w_qkv = jnp.transpose(attn_blocks[:3], (1, 0, 2))
    d_w_out = jnp.transpose(attn_blocks[3])

    dq_sum = jnp.sum(d_queries.astype(f32), axis=0)
    dv_sum = jnp.sum(dv_flat.astype(f32), axis=0)
    smalls = [
        d_lang_table, d_conv_w, d_conv_b, dq_sum, dv_sum, table_part, d_b_out, d_ln1_gain,
        d_ln1_bias, jnp.concatenate(d_bin), d_b_down, d_ln2_gain, d_ln2_bias,
    ]
    flat = lax.psum(jnp.concatenate([s.reshape(-1) for s in smalls]), ("dp", "mp"))
    back = []
    start = 0
    for s in smalls:
        back.append(flat[start : start + s.size].reshape(s.shape))
        start += s.size
    (d_lang_table, d_conv_w, d_conv_b, dq_sum, dv_sum, d_bias_table, d_b_out, d_ln1_gain,
     d_ln1_bias, d_b_in, d_b_down, d_ln2_gain, d_ln2_bias) = back
    d_b_qv = jnp.stack([
        lax.dynamic_slice_in_dim(dq_sum, mp * cols, cols),
        lax.dynamic_slice_in_dim(dv_sum, mp * cols, cols),
    ])
    d_b_in = lax.dynamic_slice_in_dim(d_b_in, mp * units, units)
    return (
        out.reshape(page_count * slots, width),
        d_tokens.reshape(page_count * slots, width),
        d_lang_table, d_conv_w, d_conv_b, d_w_qkv, d_b_qv, d_bias_table, d_w_out, d_b_out,
        d_ln1_gain, d_ln1_bias, d_w_in, d_b_in, d_w_down, d_b_down, d_ln2_gain, d_ln2_bias,
    )


def solution(mesh):
    in_specs = (
        P("dp", None), P("dp"), P("dp"),
        P("dp", "mp", None), P("dp", "mp", None), P("dp", "mp", None),
        P(), P(), P(), P(None, None, "mp"), P(None, "mp"), P(), P("mp", None),
        P(), P(), P(), P(None, "mp"), P("mp"), P("mp", None), P(), P(), P(), P("dp", None),
    )
    out_specs = (
        P("dp", None), P("dp", None), P(), P(), P(), P(None, None, "mp"), P(None, "mp"), P(),
        P("mp", None), P(), P(), P(), P(None, "mp"), P("mp"), P("mp", None), P(), P(), P(),
    )
    step = functools.partial(body, n_dp=mesh.shape["dp"], n_mp=mesh.shape["mp"])
    return jax.shard_map(step, mesh=mesh, in_specs=in_specs, out_specs=out_specs, check_vma=False)
```

time: 1180 us -> 798 us (0.68)
  matrix products: 255 us -> 75.3 us
  waiting for transfers between devices: 552 us -> 392 us
  Pallas kernels: 0 us -> 119 us
  local copies, waits for them, and re-layouts: 189 us -> 94.1 us
  other arithmetic: 113 us -> 56.2 us
  blocking collectives: 33.6 us -> 0 us
  starting transfers between devices: 12.7 us -> 39.1 us
    psum x5 -> x2, waiting for transfers between devices: 422 us -> 189 us  [the longest x1 126 us: body(): lax.psum(jnp.concatenate([s.reshape(-1) for s in smalls]), ('dp', 'mp'))]
    dot_general x62 -> x39, matrix products: 255 us -> 74.9 us  [the longest x15 36 us: dot_nn(): lax.dot_general(a, b, (((1,), (0,)), ((), ())), preferred_element_type=f32)]
    all_to_all x2 -> x0, waiting for transfers between devices: 130 us -> none  [the longest x1 130 us: body(): lax.all_to_all(row_bias, 'mp', split_axis=1, concat_axis=2, tiled=True)]
    pallas_call x0 -> x2, Pallas kernels: none -> 119 us  [the longest x1 66.7 us: attn_fwd(): pl.pallas_call(attn_fwd_kernel, out_shape=(jax.ShapeDtypeStruct(q.shape,...]
    reduce_scatter x0 -> x3, waiting for transfers between devices: none -> 110 us  [the longest x1 72.4 us: body(): lax.psum_scatter(ffn_parts, 'dp', scatter_dimension=0, tiled=False)]
    all_gather x0 -> x4, waiting for transfers between devices: none -> 77.2 us  [the longest x1 42.7 us: body(): out = lax.all_gather(out_own, 'mp', axis=1, tiled=True)]
    convert_element_type x6 -> x0, local copies, waits for them, and re-layouts: 44.5 us -> none  [the longest x2 25.1 us: body(): head_bias.astype(jnp.float32)]
    ppermute x0 -> x9, starting transfers between devices: none -> 38.3 us  [the longest x6 37.7 us: spread(): lax.ppermute(sent, 'mp', [(i, (i + s) % n_mp) for i in range(n_mp)])]
  transfers between devices with their start and end apart: 7 -> 18, of which waited for: 5 -> 10; matrix products, arithmetic and copies ran while one was open for 19% -> 20% of each run, Pallas kernels for 0% -> 8%
where the time goes in v1:
time: 798 us; the launch traced here: 791 us
  waiting for transfers between devices  392 us (49%)
  Pallas kernels  119 us (15%)
  local copies, waits for them, and re-layouts  94.1 us (12%)
  matrix products  75.3 us (9%)
  other arithmetic  56.2 us (7%)
  starting transfers between devices  39.1 us (5%)
  between operations  15.4 us (2%)
    psum x1, waiting for transfers between devices, body(): lax.psum(jnp.concatenate([s.reshape(-1) for s in smalls]), ('dp', 'mp'))  126 us
    reduce_scatter x1, waiting for transfers between devices, body(): lax.psum_scatter(ffn_parts, 'dp', scatter_dimension=0, tiled=False)  72.4 us
    pallas_call x1, Pallas kernels, attn_fwd(): pl.pallas_call(attn_fwd_kernel, out_shape=(jax.ShapeDtypeStruct(q.shape,...  66.7 us
    psum x1, waiting for transfers between devices, body(): d_tokens = lax.psum(d_tokens.astype(bf16), 'mp')  63.3 us
    pallas_call x1, Pallas kernels, attn_bwd(): pl.pallas_call(attn_bwd_kernel, out_shape=(jax.ShapeDtypeStruct(q.shape,...  52.5 us
    all_gather x1, waiting for transfers between devices, body(): out = lax.all_gather(out_own, 'mp', axis=1, tiled=True)  42.7 us
    ppermute x6, starting transfers between devices, spread(): lax.ppermute(sent, 'mp', [(i, (i + s) % n_mp) for i in range(n_mp)])  37.7 us
    dot_general x15, matrix products, dot_nn(): lax.dot_general(a, b, (((1,), (0,)), ((), ())), preferred_element_type=f32)  36 us
  transfers between devices with their start and end apart: 18, of which 10 were waited for; matrix products, arithmetic and copies ran while one was open for 20% of the time, Pallas kernels for 8%

profile of v1, /device:TPU:0, one launch (start us, length us, event | category | flops | bytes accessed | tf_op | source)
XLA Modules:
  0.0 791.2 jit_solution(17849962154486312854)
XLA Ops:
  10.7 5.1 collective-permute-start.8
  36.3 27.6 %collective-permute-start.6 = (f32[9,128]{1,0:T(8,128)S(1)}, f32[9,128]{1,0:T(8,128)S(1)}, u32[]{:S(2)}, u32[]{:S(2)}) collective-permute-start(f32[9,128]{1,0:T(8,128)S(1)} %bitcast.250), channel_id=1, source_target_pairs={{0,1},{1,2},{2,3},{3,0},{4,5},{5,6},{6,7},{7,4},{8,9},{9,10},{10,1... | collective-permute-start | bytes 13832 | tf_op jit(solution)/shard_map/ppermute | solution.py:258
  64.0 3.6 slice.400
  68.2 13.5 %collective-permute-done.2 = bf16[384,768]{1,0:T(8,128)(2,1)} collective-permute-done((bf16[384,768]{1,0:T(8,128)(2,1)}, bf16[384,768]{1,0:T(8,128)(2,1)}, u32[]{:S(2)}, u32[]{:S(2)}) %collective-permute-start.2) | collective-permute-done | bytes 589856 | tf_op jit(solution)/shard_map/ppermute | solution.py:258
  90.7 5.4 gather_fusion
  96.0 3.9 fusion.103
  103.0 3.0 convolution_convert_fusion
  106.0 3.1 add_convert_fusion
  109.0 66.7 %shard_map.358 = (bf16[352,768]{1,0:T(8,128)(2,1)}, f32[2,12,176,640]{3,2,1,0:T(8,128)}) custom-call(s32[2]{0:T(128)} %len_ref.1, bf16[352,768]{1,0:T(8,128)(2,1)} %fusion.23.q_ref, bf16[2,640,768]{2,1,0:T(8,128)(2,1)} %bitcast.192, bf16[2,640,768]{2,1,0:T(8,128)(2,1)} %bitcast.194, s32[2,176,704]{2,1,0:T(8,128)} %pos_ref.3, s32[2,176,704]{2,1,0:T(8,128)} %x_ref.3, ...), custom_call_target="tpu_custom_call" | custom-call | tf_op jit(solution)/shard_map/pallas_call | solution.py:190
  183.3 5.8 multiply_convert_fusion
  189.1 4.6 multiply_convert_fusion.1
  193.6 4.2 multiply_convert_fusion.2
  197.9 4.1 multiply_convert_fusion.3
  232.1 52.5 %shard_map.359 = (bf16[352,768]{1,0:T(8,128)(2,1)}, bf16[2,640,768]{2,1,0:T(8,128)(2,1)}, bf16[2,640,768]{2,1,0:T(8,128)(2,1)}, f32[160,12]{1,0:T(8,128)}) custom-call(bf16[352,768]{1,0:T(8,128)(2,1)} %fusion.23.q_ref, bf16[2,640,768]{2,1,0:T(8,128)(2,1)} %bitcast.193, bf16[2,640,768]{2,1,0:T(8,128)(2,1)} %bitcast.195, ...), custom_call_target="tpu_custom_call" | custom-call | tf_op jit(solution)/shard_map/pallas_call | solution.py:212
  284.6 4.6 bitcast_convert_fusion.1
  289.3 4.0 bitcast_convert_fusion
  316.1 3.7 fusion.111
  327.2 22.7 %reduce-scatter.6.cloned.1.call-done = bf16[1,4,96,768]{3,2,1,0:T(8,128)(2,1)} async-done(((bf16[8,4,96,768]{3,2,1,0:T(8,128)(2,1)}), bf16[1,4,96,768]{3,2,1,0:T(8,128)(2,1)}) %reduce-scatter.6.cloned.1.call-update) | async-done | bytes 589840 | tf_op jit(solution)/shard_map/reduce_scatter | solution.py:395
  349.9 2.9 reshape_reduce_scatter.7
  357.7 72.4 %reduce-scatter.4.cloned.1.call-done = bf16[1,8,96,768]{3,2,1,0:T(8,128)(2,1)} async-done(((bf16[8,8,96,768]{3,2,1,0:T(8,128)(2,1)}), bf16[1,8,96,768]{3,2,1,0:T(8,128)(2,1)}) %reduce-scatter.4.cloned.1.call-update) | async-done | bytes 1179664 | tf_op jit(solution)/shard_map/reduce_scatter | solution.py:394
  432.5 3.3 reshape.375
  438.7 7.4 broadcast_multiply_fusion
  446.1 11.3 %fusion.93 = (f32[768]{0:T(1024)S(1)}, f32[768]{0:T(1024)S(1)}, f32[768]{0:T(1024)S(1)}, f32[768]{0:T(1024)S(1)}, f32[2,768]{1,0:T(2,128)S(1)}, /*index=5*/bf16[2,704,768]{2,1,0:T(8,128)(2,1)}) fusion(f32[2,704,768]{2,1,0:T(8,128)} %get-tuple-element.186, f32[2,704]{1,0:T(2,128)S(1)} %compare_convert_fusion, f32[2,768]{1,0:T(2,128)S(1)} %fusion.88, ...), kind=kLoop, calls=%fused_computation.278 | loop fusion | flops 17296896 | bytes 25982464 | tf_op jit(solution)/shard_map/transpose(jvp())/reduce_sum | solution.py:300
  462.7 14.5 %reduce-scatter.8.cloned.1.call-done = bf16[1,1728,128]{2,1,0:T(8,128)(2,1)} async-done(((bf16[4,1728,128]{2,1,0:T(8,128)(2,1)}), bf16[1,1728,128]{2,1,0:T(8,128)(2,1)}) %reduce-scatter.8.cloned.1.call-update) | async-done | bytes 442384 | tf_op jit(solution)/shard_map/reduce_scatter | solution.py:401
  478.0 125.7 %all-reduce.15.cloned.1.call-done = f32[20352]{0:T(1024)} async-done(((f32[20352]{0:T(1024)}), f32[20352]{0:T(1024)}) %all-reduce.15.cloned.1.call-update) | async-done | bytes 81424 | tf_op jit(solution)/shard_map/psum | solution.py:418
  611.4 42.7 %all-gather.9.cloned.1.call-done = bf16[2,704,768]{2,1,0:T(8,128)(2,1)} async-done(((bf16[2,176,768]{2,1,0:T(8,128)(2,1)}), bf16[2,704,768]{2,1,0:T(8,128)(2,1)}) %all-gather.9.cloned.1.call-update) | async-done | bytes 2162704 | tf_op jit(solution)/shard_map/all_gather | solution.py:381
  654.1 34.5 %all-gather.11.cloned.1.call-done = bf16[8,1728,128]{2,1,0:T(8,128)(2,1)} async-done(((bf16[1,1728,128]{2,1,0:T(8,128)(2,1)}), bf16[8,1728,128]{2,1,0:T(8,128)(2,1)}) %all-gather.11.cloned.1.call-update) | async-done | bytes 3538960 | tf_op jit(solution)/shard_map/all_gather | solution.py:404
  697.2 3.0 slice.259
  701.3 4.1 slice.316
  705.4 6.0 reshape.379
  711.4 5.2 fusion.102
  716.6 63.3 %all-reduce.13.cloned.1.call-done = bf16[1408,768]{1,0:T(8,128)(2,1)} async-done(((bf16[1408,768]{1,0:T(8,128)(2,1)}), bf16[1408,768]{1,0:T(8,128)(2,1)}) %all-reduce.13.cloned.1.call-update) | async-done | bytes 2162704 | tf_op jit(solution)/shard_map/psum | solution.py:379
  (337 shorter events, 141.2 us)
Async XLA Ops:
  7.2 176.1 %all-gather.5.cloned.1.call-start = ((), (), s32[]{:S(2)}) async-start(), calls=%async_computation.3 | async-start | bytes 4866048 | tf_op jit(solution)/shard_map/all_gather | solution.py:248
  9.2 192.8 %all-gather.7.cloned.1.call-start = ((), (), s32[]{:S(2)}) async-start(), calls=%async_computation.4 | async-start | bytes 4866048 | tf_op jit(solution)/shard_map/all_gather | solution.py:249
  10.7 25.7 %collective-permute-start.8 = (f32[9,128]{1,0:T(8,128)S(1)}, f32[9,128]{1,0:T(8,128)S(1)}, u32[]{:S(2)}, u32[]{:S(2)}) collective-permute-start(f32[9,128]{1,0:T(8,128)S(1)} %bitcast.248), channel_id=1, source_target_pairs={{0,3},{1,0},{2,1},{3,2},{4,7},{5,4},{6,5},{7,6},{8,11},{9,8},{10,9... | collective-permute-start | bytes 13832 | tf_op jit(solution)/shard_map/ppermute | solution.py:258
  15.8 51.8 %collective-permute-start.7 = (f32[9,128]{1,0:T(8,128)S(1)}, f32[9,128]{1,0:T(8,128)S(1)}, u32[]{:S(2)}, u32[]{:S(2)}) collective-permute-start(f32[9,128]{1,0:T(8,128)S(1)} %bitcast.249), channel_id=1, source_target_pairs={{0,2},{1,3},{2,0},{3,1},{4,6},{5,7},{6,4},{7,5},{8,10},{9,11},{10,... | collective-permute-start | bytes 13832 | tf_op jit(solution)/shard_map/ppermute | solution.py:258
  15.8 9.0 %copy-start.14 = (bf16[768,3,192]{0,2,1:T(8,128)(2,1)S(1)}, bf16[768,3,192]{0,2,1:T(8,128)(2,1)}, u32[]{:S(2)}) copy-start(bf16[768,3,192]{0,2,1:T(8,128)(2,1)} %param.32) | copy-start | bytes 2654212
  15.8 9.0 %copy-start.31 = (bf16[192,768]{1,0:T(8,128)(2,1)S(1)}, bf16[192,768]{1,0:T(8,128)(2,1)}, u32[]{:S(2)}) copy-start(bf16[192,768]{1,0:T(8,128)(2,1)} %param.35) | copy-start | bytes 884740
  18.1 18.3 %collective-permute-start.4 = (bf16[384,768]{1,0:T(8,128)(2,1)}, bf16[384,768]{1,0:T(8,128)(2,1)}, u32[]{:S(2)}, u32[]{:S(2)}) collective-permute-start(bf16[384,768]{1,0:T(8,128)(2,1)} %fusion.79), channel_id=1, source_target_pairs={{0,3},{1,0},{2,1},{3,2},{4,7},{5,4},{6,5},{7,6},{8,11},{9,8},{10,9... | collective-permute-start | bytes 1769480 | tf_op jit(solution)/shard_map/ppermute | solution.py:258
  18.5 63.1 %collective-permute-start.2 = (bf16[384,768]{1,0:T(8,128)(2,1)}, bf16[384,768]{1,0:T(8,128)(2,1)}, u32[]{:S(2)}, u32[]{:S(2)}) collective-permute-start(bf16[384,768]{1,0:T(8,128)(2,1)} %fusion.79), channel_id=1, source_target_pairs={{0,2},{1,3},{2,0},{3,1},{4,6},{5,7},{6,4},{7,5},{8,10},{9,11},{10,... | collective-permute-start | bytes 1769480 | tf_op jit(solution)/shard_map/ppermute | solution.py:258
  21.0 61.0 %collective-permute-start = (bf16[384,768]{1,0:T(8,128)(2,1)}, bf16[384,768]{1,0:T(8,128)(2,1)}, u32[]{:S(2)}, u32[]{:S(2)}) collective-permute-start(bf16[384,768]{1,0:T(8,128)(2,1)} %fusion.79), channel_id=1, source_target_pairs={{0,1},{1,2},{2,3},{3,0},{4,5},{5,6},{6,7},{7,4},{8,9},{9,10},{10,1... | collective-permute-start | bytes 1769480 | tf_op jit(solution)/shard_map/ppermute | solution.py:258
  24.7 325.2 %reduce-scatter.6.cloned.1.call-start = ((), (), s32[]{:S(2)}) async-start(), calls=%async_computation.9 | async-start | bytes 5308416 | tf_op jit(solution)/shard_map/reduce_scatter | solution.py:395
  36.3 46.2 %collective-permute-start.5 = (bf16[384,768]{1,0:T(8,128)(2,1)}, bf16[384,768]{1,0:T(8,128)(2,1)}, u32[]{:S(2)}, u32[]{:S(2)}) collective-permute-start(bf16[384,768]{1,0:T(8,128)(2,1)} %collective-permute-done.4), channel_id=1, source_target_pairs={{0,4},{4,0},{8,12},{12,8},{16,20},{20,16},{24,28},{28,24},{1,5},{5... | collective-permute-start | bytes 1769480 | tf_op jit(solution)/shard_map/ppermute | solution.py:263
  36.3 31.2 %collective-permute-start.6 = (f32[9,128]{1,0:T(8,128)S(1)}, f32[9,128]{1,0:T(8,128)S(1)}, u32[]{:S(2)}, u32[]{:S(2)}) collective-permute-start(f32[9,128]{1,0:T(8,128)S(1)} %bitcast.250), channel_id=1, source_target_pairs={{0,1},{1,2},{2,3},{3,0},{4,5},{5,6},{6,7},{7,4},{8,9},{9,10},{10,1... | collective-permute-start | bytes 13832 | tf_op jit(solution)/shard_map/ppermute | solution.py:258
  81.7 2.3 collective-permute-start.3
  81.9 3.5 collective-permute-start.1
  99.9 6.1 copy-start.29
  99.9 6.1 copy-start.27
  181.5 44.6 %copy-start.4 = (f32[352,768]{1,0:T(8,128)}, f32[352,768]{1,0:T(8,128)S(1)}, u32[]{:S(2)}) copy-start(f32[352,768]{1,0:T(8,128)S(1)} %get-tuple-element.169) | copy-start | bytes 3244036
  183.3 5.8 copy-start.17
  183.3 5.8 copy-start.34
  214.7 8.2 %copy-start.36 = (bf16[352,768]{1,0:T(8,128)(2,1)}, bf16[352,768]{1,0:T(8,128)(2,1)S(1)}, u32[]{:S(2)}) copy-start(bf16[352,768]{1,0:T(8,128)(2,1)S(1)} %get-tuple-element.154) | copy-start | bytes 1622020
  214.8 7.2 slice-start.2
  217.5 4.5 slice-start.3
  219.7 4.9 slice-start
  284.6 4.6 copy-start.24
  297.2 132.9 %reduce-scatter.4.cloned.1.call-start = ((), (), s32[]{:S(2)}) async-start(), calls=%async_computation.8 | async-start | bytes 10616832 | tf_op jit(solution)/shard_map/reduce_scatter | solution.py:394
  315.8 161.4 %reduce-scatter.8.cloned.1.call-start = ((), (), s32[]{:S(2)}) async-start(), calls=%async_computation.10 | async-start | bytes 2211840 | tf_op jit(solution)/shard_map/reduce_scatter | solution.py:401
  438.6 165.1 %all-reduce.15.cloned.1.call-start = ((), (), s32[]{:S(2)}) async-start(), calls=%async_computation.7 | async-start | bytes 163840 | tf_op jit(solution)/shard_map/psum | solution.py:418
  438.7 7.4 copy-start.48
  461.9 192.2 %all-gather.9.cloned.1.call-start = ((), (), s32[]{:S(2)}) async-start(), calls=%async_computation.5 | async-start | bytes 2703360 | tf_op jit(solution)/shard_map/all_gather | solution.py:381
  462.7 226.0 %all-gather.11.cloned.1.call-start = ((), (), s32[]{:S(2)}) async-start(), calls=%async_computation.11 | async-start | bytes 3981312 | tf_op jit(solution)/shard_map/all_gather | solution.py:404
  477.3 302.7 %all-reduce.13.cloned.1.call-start = ((), (), s32[]{:S(2)}) async-start(), calls=%async_computation.6 | async-start | bytes 4325376 | tf_op jit(solution)/shard_map/psum | solution.py:379
  711.4 68.5 %copy-start.22 = (bf16[2,704,768]{2,1,0:T(8,128)(2,1)S(1)}, bf16[2,704,768]{2,1,0:T(8,128)(2,1)}, u32[]{:S(2)}) copy-start(bf16[2,704,768]{2,1,0:T(8,128)(2,1)} %all-gather.9.cloned.1.call-done) | copy-start | bytes 6488068
  (63 other events, 119.3 us)
Sparse Core Ops, SparseCore 0:
  11.5 94.2 all-gather.4
  108.7 61.9 all-gather.6
  297.3 52.5 reduce-scatter.5
  353.2 76.8 reduce-scatter.3
  438.7 38.4 reduce-scatter.7
  483.2 120.3 all-reduce.14
  605.3 48.8 all-gather.8
  656.0 32.6 all-gather.10
  691.6 88.2 all-reduce.12
